TPU v7x, 128 devices: a whole 4x4x4 slice. The times are simulated.
128 devices in a mesh: row: 8 (over z, core), col: 16 (over x, y).
Axes of the slice: x: 4, y: 4, z: 4, core: 2. Of those that a mesh axis runs over, the one named last changes fastest.
Arguments:
- far_field: float32 [16384, 16384], P('row', 'col'), may hold values from -4 to 4, as said below
- inverses: float32 [2, 256, 256], replicated, may hold values from -0.05 to 0.06, as said below
- test_table: float32 [524288, 128], P(('row', 'col')), may hold values from -1.5 to 1.5
- trial_table: float32 [524288, 128], P(('row', 'col')), may hold values from -1.5 to 1.5
- tile_list: int32 [2048, 2], P(('row', 'col')), may hold values from 0 to 127, as said below
- tile_nodes: int32 [2048, 256], P(('row', 'col')), may hold values from 0 to 4095
- strokes: float32 [16384, 256], P('col'), may hold values from -0.046875 to 0.046875
Outputs:
- factored: float32 [16384, 16384], P('row', 'col')
- stroke_image: float32 [16384, 256], P('row')
Inputs may be any that keep to these rules, and one draw needn't show every extreme that they name: `tile_list`: tile t lies in the block rows held by the grid row of its pair owner (owners in row-major order of the device grid). At most 2 tiles of one owner fall in the block columns of one grid column, and in every grid row some grid column receives exactly 2 tiles from every owner of that row. Duplicate blocks may occur. `tile_nodes`: node indices refer to the owner's own 4096 table rows. `far_field`: entries of order one with a dominant diagonal between 2 and 4. `inverses`: each inverse has a positive diagonal and full off-diagonal entries.
All inputs are finite; a program needn't handle non-finite values.
Results may differ from a plain program's by a relative error of at most 0.0001.
Values sent between devices are 32-bit elements; how exact they have to be, the bound alone decides.
A program may use at most 128 MiB of HBM per device.

v0:
```python
import jax
import jax.numpy as jnp
from jax import lax
from jax.sharding import PartitionSpec as P


def broadcast(value, axis, source):
    kept = jnp.where(lax.axis_index(axis) == source, value, 0).astype(value.dtype)
    return lax.psum(kept, axis)


def rows_share(block):
    return broadcast(block, "row", 0)


def on_device(far_field, inverses, test_table, trial_table, tile_list, tile_nodes, strokes):
    highest = lax.Precision.HIGHEST
    col_count = lax.axis_size("col")
    row_index = lax.axis_index("row")
    col_index = lax.axis_index("col")
    rows_local, cols_local = far_field.shape
    tile = test_table.shape[1]
    width = inverses.shape[1]
    owned = tile_list.shape[0]
    capacity = 2 * ((owned + col_count - 1) // col_count)
    block_rows = rows_local // tile
    block_cols = cols_local // tile
    left = test_table[tile_nodes]
    right = trial_table[tile_nodes]
    pieces = jnp.einsum(
        "tqi,tqj->tij", left, right, precision=highest, preferred_element_type=jnp.float32
    )
    pieces = pieces.reshape(owned, tile * tile)
    target = tile_list[:, 1] // block_cols
    position = jnp.arange(owned, dtype=jnp.int32)
    earlier = (target[None, :] == target[:, None]) & (position[None, :] < position[:, None])
    slot = target * capacity + jnp.sum(earlier.astype(jnp.int32), axis=1)
    picked = jnp.arange(col_count * capacity, dtype=jnp.int32)[:, None] == slot[None, :]
    local_block = (tile_list[:, 0] - row_index * block_rows) * block_cols + tile_list[
        :, 1
    ] % block_cols
    outgoing = jnp.dot(
        picked.astype(jnp.float32), pieces, precision=highest, preferred_element_type=jnp.float32
    )
    outgoing = outgoing.reshape(col_count, capacity, tile * tile)
    labels = jnp.sum(jnp.where(picked, local_block[None, :] + 1, 0), axis=1) - 1
    labels = labels.reshape(col_count, capacity)
    arrived, spots = (
        lax.all_to_all(outgoing, "col", split_axis=0, concat_axis=0, tiled=True),
        lax.all_to_all(labels, "col", split_axis=0, concat_axis=0, tiled=True),
    )
    arrived = arrived.reshape(col_count * capacity, tile * tile)
    spots = spots.reshape(col_count * capacity)
    placing = (
        jnp.arange(block_rows * block_cols, dtype=jnp.int32)[:, None] == spots[None, :]
    ).astype(jnp.float32)
    near = jnp.dot(placing, arrived, precision=highest, preferred_element_type=jnp.float32)
    near = (
        near.reshape(block_rows, block_cols, tile, tile)
        .transpose(0, 2, 1, 3)
        .reshape(rows_local, cols_local)
    )
    matrix = far_field + near
    global_rows = row_index * rows_local + jnp.arange(rows_local, dtype=jnp.int32)
    global_cols = col_index * cols_local + jnp.arange(cols_local, dtype=jnp.int32)
    first_grid_col = col_index == 0
    for panel in range(2):
        low = panel * width
        high = low + width
        lower = jnp.dot(
            matrix[:, low:high],
            inverses[panel],
            precision=highest,
            preferred_element_type=jnp.float32,
        )
        lower = jnp.where(global_rows[:, None] >= high, lower, 0.0)
        lower_all = broadcast(lower, "col", 0)
        upper = jnp.where(global_cols[None, :] >= high, matrix[low:high, :], 0.0)
        upper_all = rows_share(upper)
        matrix = matrix - jnp.dot(
            lower_all, upper_all, precision=highest, preferred_element_type=jnp.float32
        )
        renewed = jnp.where(global_rows[:, None] >= high, lower_all, matrix[:, low:high])
        matrix = matrix.at[:, low:high].set(jnp.where(first_grid_col, renewed, matrix[:, low:high]))
    partial_image = jnp.dot(matrix, strokes, precision=highest, preferred_element_type=jnp.float32)
    image = lax.psum(partial_image, "col")
    return (matrix, image)


def solution(mesh):
    return jax.shard_map(
        on_device,
        mesh=mesh,
        in_specs=(
            P("row", "col"),
            P(),
            P(("row", "col"), None),
            P(("row", "col"), None),
            P(("row", "col"), None),
            P(("row", "col"), None),
            P("col", None),
        ),
        out_specs=(P("row", "col"), P("row", None)),
        check_vma=False,
    )
```

profile of v0, /device:TPU:0, one launch (start us, length us, event | category | flops | bytes accessed | tf_op | source)
XLA Modules:
  0.0 573.1 jit_solution(1673368568827543794)
XLA Ops:
  9.8 7.1 %all-to-all-start = ((s32[16,1,2]{2,1,0:T(1,128)}), s32[16,1,2]{2,1,0:T(1,128)S(1)}, u32[]{:S(2)}, u32[]{:S(2)}) async-start(s32[16,1,2]{2,1,0:T(1,128)} %bitcast.3), calls=%async_computation | async-start | bytes 16384 | tf_op jit(solution)/shard_map/all_to_all | solution.py:50
  17.7 14.2 %gather_fusion = f32[4096,128]{1,0:T(8,128)} fusion(f32[4096,128]{1,0:T(8,128)S(1)} %copy-done, s32[4096]{0:T(1024)S(1)} %broadcast_clamp_fusion), kind=kCustom, calls=%fused_computation | custom fusion | bytes 4210688 | tf_op jit(solution)/shard_map/gather | solution.py:28
  31.9 15.9 %gather_fusion.1 = f32[4096,128]{1,0:T(8,128)} fusion(f32[4096,128]{1,0:T(8,128)} %param.14, s32[4096]{0:T(1024)S(1)} %broadcast_clamp_fusion), kind=kCustom, calls=%fused_computation.1 | custom fusion | bytes 4210688 | tf_op jit(solution)/shard_map/gather | solution.py:29
  47.8 5.1 fusion.31
  56.3 2.9 copy.19
  59.3 7.2 %all-to-all-start.1 = ((f32[16,2,16384]{2,1,0:T(2,128)}), f32[16,2,16384]{2,1,0:T(2,128)S(1)}, u32[]{:S(2)}, u32[]{:S(2)}) async-start(f32[16,2,16384]{2,1,0:T(2,128)} %copy.19), calls=%async_computation.1 | async-start | bytes 4194304 | tf_op jit(solution)/shard_map/all_to_all | solution.py:49
  68.0 27.8 %all-to-all-done.1 = f32[16,2,16384]{2,1,0:T(2,128)S(1)} async-done(((f32[16,2,16384]{2,1,0:T(2,128)}), f32[16,2,16384]{2,1,0:T(2,128)S(1)}, u32[]{:S(2)}, u32[]{:S(2)}) %all-to-all-start.1) | async-done | bytes 2097184 | tf_op jit(solution)/shard_map/all_to_all | solution.py:49
  95.8 2.4 reshape.215
  98.2 7.3 %fusion.4 = f32[16,8,128,128]{3,1,2,0:T(8,128)} fusion(s32[32]{0:T(128)S(1)} %eq.93, s32[16,8]{1,0:T(8,128)S(1)} %multiply_add_fusion, f32[32,16384]{1,0:T(8,128)} %reshape.215), kind=kOutput, calls=%fused_computation.14 | convolution fusion | flops 805310464 | bytes 10486400 | tf_op jit(solution)/shard_map/dot_general | solution.py:57
  105.6 12.1 %bitcast_add_fusion = f32[2048,1024]{1,0:T(8,128)} fusion(f32[2048,1024]{1,0:T(8,128)} %param.11, f32[256,8,8,128]{3,2,1,0:T(8,128)} %bitcast.63), kind=kLoop, calls=%fused_computation.2 | loop fusion | flops 2097152 | bytes 25165824 | tf_op jit(solution)/shard_map/add | solution.py:63
  117.7 2.4 fusion.9
  120.2 4.7 fusion.1
  125.9 56.5 %all-reduce.8.cloned.1.call-done = f32[256,1024]{1,0:T(8,128)} async-done(((f32[256,1024]{1,0:T(8,128)}), f32[256,1024]{1,0:T(8,128)}) %all-reduce.8.cloned.1.call-update) | async-done | bytes 1048592 | tf_op jit(solution)/shard_map/psum | solution.py:9
  182.4 94.0 %all-reduce.6.cloned.1.call-done = f32[2048,256]{1,0:T(8,128)} async-done(((f32[2048,256]{1,0:T(8,128)}), f32[2048,256]{1,0:T(8,128)}) %all-reduce.6.cloned.1.call-update) | async-done | bytes 2097168 | tf_op jit(solution)/shard_map/psum | solution.py:9
  276.5 10.6 %convolution_subtract_fusion.1 = f32[2048,1024]{1,0:T(8,128)S(1)} fusion(f32[2048,1024]{1,0:T(8,128)} %bitcast_add_fusion, f32[2048,256]{1,0:T(8,128)} %all-reduce.6.cloned.1.call-done, f32[256,1024]{1,0:T(8,128)} %all-reduce.8.cloned.1.call-done), kind=kOutput, calls=%fused_computation.4 | convolution fusion | flops 6444548096 | bytes 19922944 | tf_op jit(solution)/shard_map/dot_general | solution.py:80
  288.3 3.4 copy-done.3
  292.9 4.7 fusion
  298.6 56.8 %all-reduce.12.cloned.1.call-done = f32[256,1024]{1,0:T(8,128)} async-done(((f32[256,1024]{1,0:T(8,128)}), f32[256,1024]{1,0:T(8,128)}) %all-reduce.12.cloned.1.call-update) | async-done | bytes 1048592 | tf_op jit(solution)/shard_map/psum | solution.py:9
  355.4 93.8 %all-reduce.10.cloned.1.call-done = f32[2048,256]{1,0:T(8,128)} async-done(((f32[2048,256]{1,0:T(8,128)}), f32[2048,256]{1,0:T(8,128)}) %all-reduce.10.cloned.1.call-update) | async-done | bytes 2097168 | tf_op jit(solution)/shard_map/psum | solution.py:9
  449.3 10.6 %convolution_subtract_fusion = f32[2048,1024]{1,0:T(8,128)S(1)} fusion(f32[2048,1024]{1,0:T(8,128)} %copy-done.3, f32[2048,256]{1,0:T(8,128)} %all-reduce.10.cloned.1.call-done, f32[256,1024]{1,0:T(8,128)} %all-reduce.12.cloned.1.call-done), kind=kOutput, calls=%fused_computation.3 | convolution fusion | flops 6444548096 | bytes 19922944 | tf_op jit(solution)/shard_map/dot_general | solution.py:80
  461.3 3.4 copy-done.2
  464.7 8.3 %fusion.32 = f32[2048,256]{1,0:T(8,128)} fusion(f32[2048,1024]{1,0:T(8,128)S(1)} %fusion.3, f32[1024,256]{1,0:T(8,128)S(1)} %copy-done.7), kind=kOutput, calls=%fused_computation.69 | convolution fusion | flops 6442450944 | bytes 11534336 | tf_op jit(solution)/shard_map/dot_general | solution.py:85
  473.0 90.5 %all-reduce.14.cloned.1.call-done = f32[2048,256]{1,0:T(8,128)} async-done(((f32[2048,256]{1,0:T(8,128)}), f32[2048,256]{1,0:T(8,128)}) %all-reduce.14.cloned.1.call-update) | async-done | bytes 2097168 | tf_op jit(solution)/shard_map/psum | solution.py:86
  563.5 3.0 copy.38
  (53 shorter events, 14.1 us)
Async XLA Ops:
  7.2 10.5 %copy-start = (f32[4096,128]{1,0:T(8,128)S(1)}, f32[4096,128]{1,0:T(8,128)}, u32[]{:S(2)}) copy-start(f32[4096,128]{1,0:T(8,128)} %param.13) | copy-start | bytes 6291460
  9.8 49.5 %all-to-all-start = ((s32[16,1,2]{2,1,0:T(1,128)}), s32[16,1,2]{2,1,0:T(1,128)S(1)}, u32[]{:S(2)}, u32[]{:S(2)}) async-start(s32[16,1,2]{2,1,0:T(1,128)} %bitcast.3), calls=%async_computation | async-start | bytes 16384 | tf_op jit(solution)/shard_map/all_to_all | solution.py:50
  31.9 15.9 %copy-start.6 = (f32[4096,128]{1,0:T(8,128)S(1)}, f32[4096,128]{1,0:T(8,128)}, u32[]{:S(2)}) copy-start(f32[4096,128]{1,0:T(8,128)} %gather_fusion) | copy-start | bytes 6291460
  59.3 36.5 %all-to-all-start.1 = ((f32[16,2,16384]{2,1,0:T(2,128)}), f32[16,2,16384]{2,1,0:T(2,128)S(1)}, u32[]{:S(2)}, u32[]{:S(2)}) async-start(f32[16,2,16384]{2,1,0:T(2,128)} %copy.19), calls=%async_computation.1 | async-start | bytes 4194304 | tf_op jit(solution)/shard_map/all_to_all | solution.py:49
  66.5 115.9 %all-reduce.8.cloned.1.call-start = ((), (), s32[]{:S(2)}) async-start(), calls=%async_computation.3 | async-start | bytes 2097152 | tf_op jit(solution)/shard_map/psum | solution.py:9
  117.7 2.5 copy-start.8
  120.1 156.3 %all-reduce.6.cloned.1.call-start = ((), (), s32[]{:S(2)}) async-start(), calls=%async_computation.2 | async-start | bytes 4194304 | tf_op jit(solution)/shard_map/psum | solution.py:9
  125.0 230.5 %all-reduce.12.cloned.1.call-start = ((), (), s32[]{:S(2)}) async-start(), calls=%async_computation.5 | async-start | bytes 2097152 | tf_op jit(solution)/shard_map/psum | solution.py:9
  276.5 10.6 %copy-start.4 = (f32[2048,256]{1,0:T(8,128)S(1)}, f32[2048,256]{1,0:T(8,128)}, u32[]{:S(2)}) copy-start(f32[2048,256]{1,0:T(8,128)} %all-reduce.6.cloned.1.call-done) | copy-start | bytes 6291460
  288.3 3.4 copy-start.3
  292.9 156.4 %all-reduce.10.cloned.1.call-start = ((), (), s32[]{:S(2)}) async-start(), calls=%async_computation.4 | async-start | bytes 4194304 | tf_op jit(solution)/shard_map/psum | solution.py:9
  297.7 265.8 %all-reduce.14.cloned.1.call-start = ((), (), s32[]{:S(2)}) async-start(), calls=%async_computation.6 | async-start | bytes 4194304 | tf_op jit(solution)/shard_map/psum | solution.py:86
  449.3 10.6 %copy-start.5 = (f32[2048,256]{1,0:T(8,128)S(1)}, f32[2048,256]{1,0:T(8,128)}, u32[]{:S(2)}) copy-start(f32[2048,256]{1,0:T(8,128)} %all-reduce.10.cloned.1.call-done) | copy-start | bytes 6291460
  459.9 4.8 copy-start.7
  461.2 3.4 copy-start.2
  472.9 93.6 %copy-start.1 = (f32[4096,128]{1,0:T(8,128)S(1)}, f32[4096,128]{1,0:T(8,128)}, u32[]{:S(2)}) copy-start(f32[4096,128]{1,0:T(8,128)} %param.13) | copy-start | bytes 6291460
Sparse Core Ops, SparseCore 0:
  120.3 62.1 all-reduce.7
  186.3 90.0 all-reduce.5
  293.0 62.3 all-reduce.11
  359.2 90.0 all-reduce.9
  473.1 90.3 all-reduce.13
where the time goes:
time: 574 us; the launch traced here: 573 us
  waiting for transfers between devices  420 us (73%)
  matrix products  53.5 us (9%)
  local copies, waits for them, and re-layouts  47.8 us (8%)
  other arithmetic  23 us (4%)
  starting transfers between devices  15.2 us (3%)
  between operations  14 us (2%)
    psum x4, waiting for transfers between devices, broadcast(): return lax.psum(kept, axis)  301 us
    psum x1, waiting for transfers between devices, on_device(): image = lax.psum(partial_image, 'col')  90.5 us
    all_to_all x1, waiting for transfers between devices, on_device(): lax.all_to_all(outgoing, 'col', split_axis=0, concat_axis=0, tiled=True)  27.8 us
    dot_general x2, matrix products, on_device(): jnp.dot(lower_all, upper_all, precision=highest, preferred_element_type=j...  21.1 us
    gather x1, local copies, waits for them, and re-layouts, on_device(): right = trial_table[tile_nodes]  15.9 us
    gather x1, local copies, waits for them, and re-layouts, on_device(): left = test_table[tile_nodes]  14.2 us
    add x1, other arithmetic, on_device(): matrix = far_field + near  12.1 us
  transfers between devices with their start and end apart: 7, of which 6 were waited for; matrix products, arithmetic and copies ran while one was open for 9% of the time, Pallas kernels for 0%

commit v1 on v0

--- a/solution.py
+++ b/solution.py
@@ -83,7 +83,9 @@
         renewed = jnp.where(global_rows[:, None] >= high, lower_all, matrix[:, low:high])
         matrix = matrix.at[:, low:high].set(jnp.where(first_grid_col, renewed, matrix[:, low:high]))
     partial_image = jnp.dot(matrix, strokes, precision=highest, preferred_element_type=jnp.float32)
-    image = lax.psum(partial_image, "col")
+    image = partial_image
+    for hop in (1, 2, 4, 8):
+        image = image + lax.ppermute(image, "col", [(dev, dev ^ hop) for dev in range(16)])
     return (matrix, image)
 
 

time: 574 us -> 660 us (1.15)
  waiting for transfers between devices: 420 us -> 508 us
    ppermute x0 -> x4, waiting for transfers between devices: none -> 179 us  [on_device(): lax.ppermute(image, 'col', [(dev, dev ^ hop) for dev in range(16)])]
    psum x1 -> x0, waiting for transfers between devices: 90.5 us -> none  [on_device(): image = lax.psum(partial_image, 'col')]
  transfers between devices with their start and end apart: 7 -> 10, of which waited for: 6 -> 9; matrix products, arithmetic and copies ran while one was open for 9% -> 8% of each run, Pallas kernels for 0% -> 0%
where the time goes in v1:
time: 660 us; the launch traced here: 659 us
  waiting for transfers between devices  508 us (77%)
  matrix products  52.2 us (8%)
  local copies, waits for them, and re-layouts  41.4 us (6%)
  other arithmetic  25.5 us (4%)
  starting transfers between devices  17.5 us (3%)
  between operations  14 us (2%)
    psum x4, waiting for transfers between devices, broadcast(): return lax.psum(kept, axis)  302 us
    ppermute x4, waiting for transfers between devices, on_device(): lax.ppermute(image, 'col', [(dev, dev ^ hop) for dev in range(16)])  179 us
    all_to_all x1, waiting for transfers between devices, on_device(): lax.all_to_all(outgoing, 'col', split_axis=0, concat_axis=0, tiled=True)  27.8 us
    dot_general x2, matrix products, on_device(): jnp.dot(lower_all, upper_all, precision=highest, preferred_element_type=j...  21.1 us
    gather x1, local copies, waits for them, and re-layouts, on_device(): right = trial_table[tile_nodes]  15.9 us
    gather x1, local copies, waits for them, and re-layouts, on_device(): left = test_table[tile_nodes]  14.2 us
  transfers between devices with their start and end apart: 10, of which 9 were waited for; matrix products, arithmetic and copies ran while one was open for 8% of the time, Pallas kernels for 0%

profile of v1, /device:TPU:0, one launch (start us, length us, event | category | flops | bytes accessed | tf_op | source)
XLA Modules:
  0.0 659.1 jit_solution(15547132734922509253)
XLA Ops:
  9.8 7.1 %all-to-all-start = ((s32[16,1,2]{2,1,0:T(1,128)}), s32[16,1,2]{2,1,0:T(1,128)S(1)}, u32[]{:S(2)}, u32[]{:S(2)}) async-start(s32[16,1,2]{2,1,0:T(1,128)} %bitcast.3), calls=%async_computation | async-start | bytes 16384 | tf_op jit(solution)/shard_map/all_to_all | solution.py:50
  17.7 14.2 %gather_fusion = f32[4096,128]{1,0:T(8,128)} fusion(f32[4096,128]{1,0:T(8,128)S(1)} %copy-done, s32[4096]{0:T(1024)S(1)} %broadcast_clamp_fusion), kind=kCustom, calls=%fused_computation | custom fusion | bytes 4210688 | tf_op jit(solution)/shard_map/gather | solution.py:28
  31.9 15.9 %gather_fusion.1 = f32[4096,128]{1,0:T(8,128)} fusion(f32[4096,128]{1,0:T(8,128)} %param.14, s32[4096]{0:T(1024)S(1)} %broadcast_clamp_fusion), kind=kCustom, calls=%fused_computation.1 | custom fusion | bytes 4210688 | tf_op jit(solution)/shard_map/gather | solution.py:29
  47.8 5.1 fusion.31
  56.3 2.9 copy.19
  59.3 7.2 %all-to-all-start.1 = ((f32[16,2,16384]{2,1,0:T(2,128)}), f32[16,2,16384]{2,1,0:T(2,128)S(1)}, u32[]{:S(2)}, u32[]{:S(2)}) async-start(f32[16,2,16384]{2,1,0:T(2,128)} %copy.19), calls=%async_computation.1 | async-start | bytes 4194304 | tf_op jit(solution)/shard_map/all_to_all | solution.py:49
  68.0 27.8 %all-to-all-done.1 = f32[16,2,16384]{2,1,0:T(2,128)S(1)} async-done(((f32[16,2,16384]{2,1,0:T(2,128)}), f32[16,2,16384]{2,1,0:T(2,128)S(1)}, u32[]{:S(2)}, u32[]{:S(2)}) %all-to-all-start.1) | async-done | bytes 2097184 | tf_op jit(solution)/shard_map/all_to_all | solution.py:49
  98.2 7.3 %fusion.4 = f32[16,8,128,128]{3,1,2,0:T(8,128)} fusion(s32[32]{0:T(128)S(1)} %eq.93, s32[16,8]{1,0:T(8,128)S(1)} %multiply_add_fusion, f32[32,16384]{1,0:T(8,128)} %reshape.215), kind=kOutput, calls=%fused_computation.14 | convolution fusion | flops 805310464 | bytes 10486400 | tf_op jit(solution)/shard_map/dot_general | solution.py:57
  105.6 12.1 %bitcast_add_fusion = f32[2048,1024]{1,0:T(8,128)} fusion(f32[2048,1024]{1,0:T(8,128)} %param.11, f32[256,8,8,128]{3,2,1,0:T(8,128)} %bitcast.63), kind=kLoop, calls=%fused_computation.2 | loop fusion | flops 2097152 | bytes 25165824 | tf_op jit(solution)/shard_map/add | solution.py:63
  117.7 2.4 fusion.9
  120.2 4.7 fusion.1
  125.7 56.8 %all-reduce.7.cloned.1.call-done = f32[256,1024]{1,0:T(8,128)} async-done(((f32[256,1024]{1,0:T(8,128)}), f32[256,1024]{1,0:T(8,128)}) %all-reduce.7.cloned.1.call-update) | async-done | bytes 1048592 | tf_op jit(solution)/shard_map/psum | solution.py:9
  182.4 94.0 %all-reduce.5.cloned.1.call-done = f32[2048,256]{1,0:T(8,128)} async-done(((f32[2048,256]{1,0:T(8,128)}), f32[2048,256]{1,0:T(8,128)}) %all-reduce.5.cloned.1.call-update) | async-done | bytes 2097168 | tf_op jit(solution)/shard_map/psum | solution.py:9
  276.5 10.6 %convolution_subtract_fusion.1 = f32[2048,1024]{1,0:T(8,128)S(1)} fusion(f32[2048,1024]{1,0:T(8,128)} %bitcast_add_fusion, f32[2048,256]{1,0:T(8,128)} %all-reduce.5.cloned.1.call-done, f32[256,1024]{1,0:T(8,128)} %all-reduce.7.cloned.1.call-done), kind=kOutput, calls=%fused_computation.4 | convolution fusion | flops 6444548096 | bytes 19922944 | tf_op jit(solution)/shard_map/dot_general | solution.py:80
  288.3 3.4 copy-done.3
  293.0 4.7 fusion
  298.5 56.9 %all-reduce.11.cloned.1.call-done = f32[256,1024]{1,0:T(8,128)} async-done(((f32[256,1024]{1,0:T(8,128)}), f32[256,1024]{1,0:T(8,128)}) %all-reduce.11.cloned.1.call-update) | async-done | bytes 1048592 | tf_op jit(solution)/shard_map/psum | solution.py:9
  355.4 93.9 %all-reduce.9.cloned.1.call-done = f32[2048,256]{1,0:T(8,128)} async-done(((f32[2048,256]{1,0:T(8,128)}), f32[2048,256]{1,0:T(8,128)}) %all-reduce.9.cloned.1.call-update) | async-done | bytes 2097168 | tf_op jit(solution)/shard_map/psum | solution.py:9
  449.3 10.6 %convolution_subtract_fusion = f32[2048,1024]{1,0:T(8,128)S(1)} fusion(f32[2048,1024]{1,0:T(8,128)} %copy-done.3, f32[2048,256]{1,0:T(8,128)} %all-reduce.9.cloned.1.call-done, f32[256,1024]{1,0:T(8,128)} %all-reduce.11.cloned.1.call-done), kind=kOutput, calls=%fused_computation.3 | convolution fusion | flops 6444548096 | bytes 19922944 | tf_op jit(solution)/shard_map/dot_general | solution.py:80
  461.3 7.0 %fusion.32 = f32[2048,256]{1,0:T(8,128)S(1)} fusion(f32[2048,1024]{1,0:T(8,128)S(1)} %fusion.3, f32[1024,256]{1,0:T(8,128)S(1)} %copy-done.7), kind=kOutput, calls=%fused_computation.69 | convolution fusion | flops 6442450944 | bytes 11534336 | tf_op jit(solution)/shard_map/dot_general | solution.py:85
  469.5 45.0 %collective-permute-done = f32[2048,256]{1,0:T(8,128)S(1)} collective-permute-done((f32[2048,256]{1,0:T(8,128)S(1)}, f32[2048,256]{1,0:T(8,128)S(1)}, u32[]{:S(2)}, u32[]{:S(2)}) %collective-permute-start) | collective-permute-done | bytes 2097184 | tf_op jit(solution)/shard_map/ppermute | solution.py:88
  516.2 45.2 %collective-permute-done.1 = f32[2048,256]{1,0:T(8,128)S(1)} collective-permute-done((f32[2048,256]{1,0:T(8,128)S(1)}, f32[2048,256]{1,0:T(8,128)S(1)}, u32[]{:S(2)}, u32[]{:S(2)}) %collective-permute-start.1) | collective-permute-done | bytes 2097184 | tf_op jit(solution)/shard_map/ppermute | solution.py:88
  561.7 46.3 %collective-permute-done.2 = f32[2048,256]{1,0:T(8,128)S(1)} collective-permute-done((f32[2048,256]{1,0:T(8,128)S(1)}, f32[2048,256]{1,0:T(8,128)S(1)}, u32[]{:S(2)}, u32[]{:S(2)}) %collective-permute-start.2) | collective-permute-done | bytes 2097184 | tf_op jit(solution)/shard_map/ppermute | solution.py:88
  608.4 42.5 %collective-permute-done.3 = f32[2048,256]{1,0:T(8,128)S(1)} collective-permute-done((f32[2048,256]{1,0:T(8,128)S(1)}, f32[2048,256]{1,0:T(8,128)S(1)}, u32[]{:S(2)}, u32[]{:S(2)}) %collective-permute-start.3) | collective-permute-done | bytes 2097184 | tf_op jit(solution)/shard_map/ppermute | solution.py:88
  (61 shorter events, 21.3 us)
Async XLA Ops:
  7.2 10.5 %copy-start = (f32[4096,128]{1,0:T(8,128)S(1)}, f32[4096,128]{1,0:T(8,128)}, u32[]{:S(2)}) copy-start(f32[4096,128]{1,0:T(8,128)} %param.13) | copy-start | bytes 6291460
  9.8 49.5 %all-to-all-start = ((s32[16,1,2]{2,1,0:T(1,128)}), s32[16,1,2]{2,1,0:T(1,128)S(1)}, u32[]{:S(2)}, u32[]{:S(2)}) async-start(s32[16,1,2]{2,1,0:T(1,128)} %bitcast.3), calls=%async_computation | async-start | bytes 16384 | tf_op jit(solution)/shard_map/all_to_all | solution.py:50
  31.9 15.9 %copy-start.6 = (f32[4096,128]{1,0:T(8,128)S(1)}, f32[4096,128]{1,0:T(8,128)}, u32[]{:S(2)}) copy-start(f32[4096,128]{1,0:T(8,128)} %gather_fusion) | copy-start | bytes 6291460
  59.3 36.5 %all-to-all-start.1 = ((f32[16,2,16384]{2,1,0:T(2,128)}), f32[16,2,16384]{2,1,0:T(2,128)S(1)}, u32[]{:S(2)}, u32[]{:S(2)}) async-start(f32[16,2,16384]{2,1,0:T(2,128)} %copy.19), calls=%async_computation.1 | async-start | bytes 4194304 | tf_op jit(solution)/shard_map/all_to_all | solution.py:49
  66.5 115.9 %all-reduce.7.cloned.1.call-start = ((), (), s32[]{:S(2)}) async-start(), calls=%async_computation.3 | async-start | bytes 2097152 | tf_op jit(solution)/shard_map/psum | solution.py:9
  117.7 2.5 copy-start.8
  120.1 156.3 %all-reduce.5.cloned.1.call-start = ((), (), s32[]{:S(2)}) async-start(), calls=%async_computation.2 | async-start | bytes 4194304 | tf_op jit(solution)/shard_map/psum | solution.py:9
  125.0 230.5 %all-reduce.11.cloned.1.call-start = ((), (), s32[]{:S(2)}) async-start(), calls=%async_computation.5 | async-start | bytes 2097152 | tf_op jit(solution)/shard_map/psum | solution.py:9
  276.5 10.6 %copy-start.4 = (f32[2048,256]{1,0:T(8,128)S(1)}, f32[2048,256]{1,0:T(8,128)}, u32[]{:S(2)}) copy-start(f32[2048,256]{1,0:T(8,128)} %all-reduce.5.cloned.1.call-done) | copy-start | bytes 6291460
  288.3 3.4 copy-start.3
  292.9 156.4 %all-reduce.9.cloned.1.call-start = ((), (), s32[]{:S(2)}) async-start(), calls=%async_computation.4 | async-start | bytes 4194304 | tf_op jit(solution)/shard_map/psum | solution.py:9
  449.3 10.6 %copy-start.5 = (f32[2048,256]{1,0:T(8,128)S(1)}, f32[2048,256]{1,0:T(8,128)}, u32[]{:S(2)}) copy-start(f32[2048,256]{1,0:T(8,128)} %all-reduce.9.cloned.1.call-done) | copy-start | bytes 6291460
  459.9 1.3 copy-start.7
  461.2 7.0 %copy-start.2 = (f32[2048,1024]{1,0:T(8,128)}, f32[2048,1024]{1,0:T(8,128)S(1)}, u32[]{:S(2)}) copy-start(f32[2048,1024]{1,0:T(8,128)S(1)} %fusion.3) | copy-start | bytes 25165828
  468.2 46.3 %collective-permute-start = (f32[2048,256]{1,0:T(8,128)S(1)}, f32[2048,256]{1,0:T(8,128)S(1)}, u32[]{:S(2)}, u32[]{:S(2)}) collective-permute-start(f32[2048,256]{1,0:T(8,128)S(1)} %fusion.32), channel_id=1, source_target_pairs={{0,1},{1,0},{2,3},{3,2},{4,5},{5,4},{6,7},{7,6},{8,9},{9,8},{10,11... | collective-permute-start | bytes 6291464 | tf_op jit(solution)/shard_map/ppermute | solution.py:88
  514.8 46.6 %collective-permute-start.1 = (f32[2048,256]{1,0:T(8,128)S(1)}, f32[2048,256]{1,0:T(8,128)S(1)}, u32[]{:S(2)}, u32[]{:S(2)}) collective-permute-start(f32[2048,256]{1,0:T(8,128)S(1)} %add.126), channel_id=1, source_target_pairs={{0,2},{1,3},{2,0},{3,1},{4,6},{5,7},{6,4},{7,5},{8,10},{9,11},{10,... | collective-permute-start | bytes 6291464 | tf_op jit(solution)/shard_map/ppermute | solution.py:88
  561.6 46.4 %collective-permute-start.2 = (f32[2048,256]{1,0:T(8,128)S(1)}, f32[2048,256]{1,0:T(8,128)S(1)}, u32[]{:S(2)}, u32[]{:S(2)}) collective-permute-start(f32[2048,256]{1,0:T(8,128)S(1)} %add.127), channel_id=1, source_target_pairs={{0,4},{1,5},{2,6},{3,7},{4,0},{5,1},{6,2},{7,3},{8,12},{9,13},{10,... | collective-permute-start | bytes 6291464 | tf_op jit(solution)/shard_map/ppermute | solution.py:88
  608.1 44.5 %copy-start.1 = (f32[4096,128]{1,0:T(8,128)S(1)}, f32[4096,128]{1,0:T(8,128)}, u32[]{:S(2)}) copy-start(f32[4096,128]{1,0:T(8,128)} %param.13) | copy-start | bytes 6291460
  608.3 42.6 %collective-permute-start.3 = (f32[2048,256]{1,0:T(8,128)S(1)}, f32[2048,256]{1,0:T(8,128)S(1)}, u32[]{:S(2)}, u32[]{:S(2)}) collective-permute-start(f32[2048,256]{1,0:T(8,128)S(1)} %add.128), channel_id=1, source_target_pairs={{0,8},{1,9},{2,10},{3,11},{4,12},{5,13},{6,14},{7,15},{8,0},{9,1},... | collective-permute-start | bytes 6291464 | tf_op jit(solution)/shard_map/ppermute | solution.py:88
Sparse Core Ops, SparseCore 0:
  120.3 62.1 all-reduce.6
  186.3 90.0 all-reduce.4
  293.0 62.3 all-reduce.10
  359.2 90.0 all-reduce.8
